TPU v7x, 128 devices: a whole 4x4x4 slice. The times are simulated.
128 devices in a mesh: row: 16 (over y, z), col: 8 (over x, core).
Axes of the slice: x: 4, y: 4, z: 4, core: 2. Of those that a mesh axis runs over, the one named last changes fastest.
Arguments:
- tokens: bfloat16 [2048, 4096], P('row', 'col'), may hold values from -6 to 6
- w_in: bfloat16 [4096, 16384], P('col', 'row'), may hold values from -0.09375 to 0.09375
- w_out: bfloat16 [16384, 4096], P('row', 'col'), may hold values from -0.046875 to 0.046875
- cotangent: bfloat16 [2048, 4096], P('row', 'col'), may hold values from -6 to 6
Outputs:
- block_out: bfloat16 [2048, 4096], P(('row', 'col'))
- grad_tokens: bfloat16 [2048, 4096], P('row', 'col')
- grad_in: float32 [4096, 16384], P('col', 'row')
- grad_out: float32 [16384, 4096], P('row', 'col')
All inputs are finite; a program needn't handle non-finite values.
Results may differ from a plain program's by a relative error of at most 0.015.
Values may be sent and summed in bfloat16 or wider, within the bound.
A program may use at most 128 MiB of HBM per device.

v0:
```python
import jax
import jax.numpy as jnp
from jax import lax
from jax.sharding import PartitionSpec as P


def gelu_grad(value):
    cdf = 0.5 * (1.0 + jax.scipy.special.erf(value * 0.7071067811865476))
    pdf = jnp.exp(-0.5 * value * value) * 0.3989422804014327
    return cdf + value * pdf


def token_panel(local_rows):
    return lax.all_gather(local_rows, "row", axis=0, tiled=True)


def hidden_panel(local_rows):
    return lax.all_gather(local_rows, "col", axis=0, tiled=True)


def contract_last(left, right):
    return lax.dot_general(
        left, right, (((1,), (1,)), ((), ())), preferred_element_type=jnp.float32
    )


def width_split(left_all, right, transposed):

    def width_term():
        if transposed:
            return contract_last(left_all, right)
        return jnp.dot(left_all, right, preferred_element_type=jnp.float32)

    return lax.psum_scatter(
        width_term().astype(jnp.bfloat16), "col", scatter_dimension=0, tiled=True
    ).astype(jnp.float32)


def unit_sum(left_all, right, transposed):

    def unit_term():
        if transposed:
            return contract_last(left_all, right)
        return jnp.dot(left_all, right, preferred_element_type=jnp.float32)

    return lax.psum_scatter(
        unit_term().astype(jnp.bfloat16), "row", scatter_dimension=0, tiled=True
    ).astype(jnp.float32)


def local(tokens, w_in, w_out, cotangent):
    tokens_all = token_panel(tokens)
    upstream_all = token_panel(cotangent)
    pre_part = width_split(tokens_all, w_in, False)
    act_all = hidden_panel(jax.nn.gelu(pre_part, approximate=False).astype(jnp.bfloat16))
    dact_part = width_split(upstream_all, w_out, True)
    dpre_all = hidden_panel((dact_part * gelu_grad(pre_part)).astype(jnp.bfloat16))
    mixed = unit_sum(act_all, w_out, False)
    block_rows = (tokens.astype(jnp.float32) + mixed).astype(jnp.bfloat16)
    block_out = lax.all_to_all(block_rows, "col", split_axis=0, concat_axis=1, tiled=True)
    grad_out = lax.dot_general(
        act_all, upstream_all, (((0,), (0,)), ((), ())), preferred_element_type=jnp.float32
    )
    grad_in = lax.dot_general(
        tokens_all, dpre_all, (((0,), (0,)), ((), ())), preferred_element_type=jnp.float32
    )
    back = unit_sum(dpre_all, w_in, True)
    grad_tokens = (cotangent.astype(jnp.float32) + back).astype(jnp.bfloat16)
    return (block_out, grad_tokens, grad_in, grad_out)


def solution(mesh):
    in_specs = (P("row", "col"), P("col", "row"), P("row", "col"), P("row", "col"))
    out_specs = (P(("row", "col"), None), P("row", "col"), P("col", "row"), P("row", "col"))
    return jax.shard_map(local, mesh=mesh, in_specs=in_specs, out_specs=out_specs, check_vma=False)
```

profile of v0, /device:TPU:0, one launch (start us, length us, event | category | flops | bytes accessed | tf_op | source)
XLA Modules:
  0.0 417.5 jit_solution(6592428128549312227)
XLA Ops:
  7.2 0.0 copy-start
  7.2 0.0 all-gather.9.cloned.1.call-start
  7.2 0.7 all-gather.9.cloned.1.call-update
  7.9 0.0 all-gather.5.cloned.1.call-start
  8.0 0.7 all-gather.5.cloned.1.call-update
  8.7 0.0 reduce-scatter.9.cloned.1.call-start
  8.7 49.2 %all-gather.9.cloned.1.call-done = bf16[2048,512]{1,0:T(8,128)(2,1)} async-done(((bf16[128,512]{1,0:T(8,128)(2,1)}), bf16[2048,512]{1,0:T(8,128)(2,1)}) %all-gather.9.cloned.1.call-update) | async-done | bytes 2097168 | tf_op jit(solution)/shard_map/all_gather | solution.py:14
  58.0 0.0 copy-done
  58.0 5.9 %convolution_convert_fusion = bf16[2048,1024]{1,0:T(8,128)(2,1)} fusion(bf16[2048,512]{1,0:T(8,128)(2,1)} %all-gather.9.cloned.1.call-done, bf16[1024,512]{1,0:T(8,128)(2,1)S(1)} %copy-done), kind=kOutput, calls=%fused_computation | convolution fusion | flops 2149580800 | bytes 7340032 | tf_op jit(solution)/shard_map/dot_general | solution.py:22
  63.9 0.0 copy-start.3
  63.9 0.0 reduce-scatter.9.cloned.1.call-update
  63.9 0.0 reduce-scatter.5.cloned.1.call-start
  64.0 40.7 %all-gather.5.cloned.1.call-done = bf16[2048,512]{1,0:T(8,128)(2,1)} async-done(((bf16[128,512]{1,0:T(8,128)(2,1)}), bf16[2048,512]{1,0:T(8,128)(2,1)}) %all-gather.5.cloned.1.call-update) | async-done | bytes 2097168 | tf_op jit(solution)/shard_map/all_gather | solution.py:14
  104.7 0.0 copy-done.3
  104.7 5.9 %convolution_convert_fusion.1 = bf16[2048,1024]{1,0:T(8,128)(2,1)} fusion(bf16[2048,512]{1,0:T(8,128)(2,1)} %all-gather.5.cloned.1.call-done, bf16[512,1024]{1,0:T(8,128)(2,1)S(1)} %copy-done.3), kind=kOutput, calls=%fused_computation.1 | convolution fusion | flops 2149580800 | bytes 7340032 | tf_op jit(solution)/shard_map/dot_general | solution.py:32
  110.6 0.0 reduce-scatter.5.cloned.1.call-update
  110.6 0.0 all-gather.7.cloned.1.call-start
  110.7 33.6 %reduce-scatter.9.cloned.1.call-done = bf16[256,1024]{1,0:T(8,128)(2,1)} async-done(((bf16[2048,1024]{1,0:T(8,128)(2,1)}), bf16[256,1024]{1,0:T(8,128)(2,1)}) %reduce-scatter.9.cloned.1.call-update) | async-done | bytes 524304 | tf_op jit(solution)/shard_map/reduce_scatter | solution.py:34
  144.2 38.9 %reduce-scatter.5.cloned.1.call-done = bf16[256,1024]{1,0:T(8,128)(2,1)} async-done(((bf16[2048,1024]{1,0:T(8,128)(2,1)}), bf16[256,1024]{1,0:T(8,128)(2,1)}) %reduce-scatter.5.cloned.1.call-update) | async-done | bytes 524304 | tf_op jit(solution)/shard_map/reduce_scatter | solution.py:34
  183.2 4.6 %fusion.38 = (bf16[256,1024]{1,0:T(8,128)(2,1)}, bf16[256,1024]{1,0:T(8,128)(2,1)}) fusion(bf16[256,1024]{1,0:T(8,128)(2,1)} %reduce-scatter.5.cloned.1.call-done, bf16[256,1024]{1,0:T(8,128)(2,1)} %reduce-scatter.9.cloned.1.call-done), kind=kLoop, calls=%fused_computation.50 | loop fusion | flops 20185088 | bytes 2097152 | tf_op jit(solution)/shard_map/convert_element_type | solution.py:57
  187.7 0.0 all-gather.7.cloned.1.call-update
  187.8 0.0 all-gather.11.cloned.1.call-start
  187.8 0.5 all-gather.11.cloned.1.call-update
  188.3 0.0 reduce-scatter.7.cloned.1.call-start
  188.4 30.6 %all-gather.7.cloned.1.call-done = bf16[2048,1024]{1,0:T(8,128)(2,1)} async-done(((bf16[256,1024]{1,0:T(8,128)(2,1)}), bf16[2048,1024]{1,0:T(8,128)(2,1)}) %all-gather.7.cloned.1.call-update) | async-done | bytes 4194320 | tf_op jit(solution)/shard_map/all_gather | solution.py:18
  219.0 5.9 %convolution_convert_fusion.3 = bf16[2048,512]{1,0:T(8,128)(2,1)} fusion(bf16[2048,1024]{1,0:T(8,128)(2,1)} %all-gather.7.cloned.1.call-done, bf16[1024,512]{1,0:T(8,128)(2,1)S(1)} %copy-done), kind=kOutput, calls=%fused_computation.3 | convolution fusion | flops 2148532224 | bytes 7340032 | tf_op jit(solution)/shard_map/dot_general | solution.py:44
  224.9 0.0 reduce-scatter.7.cloned.1.call-update
  224.9 0.2 reduce-scatter.11.cloned.1.call-start
  225.2 28.1 %all-gather.11.cloned.1.call-done = bf16[2048,1024]{1,0:T(8,128)(2,1)} async-done(((bf16[256,1024]{1,0:T(8,128)(2,1)}), bf16[2048,1024]{1,0:T(8,128)(2,1)}) %all-gather.11.cloned.1.call-update) | async-done | bytes 4194320 | tf_op jit(solution)/shard_map/all_gather | solution.py:18
  253.2 5.9 %convolution_convert_fusion.2 = bf16[2048,512]{1,0:T(8,128)(2,1)} fusion(bf16[2048,1024]{1,0:T(8,128)(2,1)} %all-gather.11.cloned.1.call-done, bf16[512,1024]{1,0:T(8,128)(2,1)S(1)} %copy-done.3), kind=kOutput, calls=%fused_computation.2 | convolution fusion | flops 2148532224 | bytes 7340032 | tf_op jit(solution)/shard_map/dot_general | solution.py:22
  259.1 0.0 reduce-scatter.11.cloned.1.call-update
  259.1 5.2 %convolution_bitcast_fusion = f32[512,1024]{0,1:T(8,128)S(1)} fusion(bf16[2048,1024]{1,0:T(8,128)(2,1)} %all-gather.11.cloned.1.call-done, bf16[2048,512]{1,0:T(8,128)(2,1)} %all-gather.5.cloned.1.call-done), kind=kOutput, calls=%fused_computation.10 | convolution fusion | flops 2147483648 | bytes 8388608 | tf_op jit(solution)/shard_map/dot_general | solution.py:64
  264.4 1.8 copy.9
  266.2 0.0 copy-start.1
  266.2 0.0 copy-start.2
  266.2 6.6 %fusion.39 = f32[1024,512]{1,0:T(8,128)} fusion(bf16[2048,1024]{1,0:T(8,128)(2,1)} %all-gather.7.cloned.1.call-done, bf16[2048,512]{1,0:T(8,128)(2,1)} %all-gather.9.cloned.1.call-done), kind=kOutput, calls=%fused_computation.53 | convolution fusion | flops 2147483648 | bytes 8388608 | tf_op jit(solution)/shard_map/dot_general | solution.py:61
  272.8 58.3 %reduce-scatter.7.cloned.1.call-done = bf16[128,512]{1,0:T(8,128)(2,1)} async-done(((bf16[2048,512]{1,0:T(8,128)(2,1)}), bf16[128,512]{1,0:T(8,128)(2,1)}) %reduce-scatter.7.cloned.1.call-update) | async-done | bytes 131088 | tf_op jit(solution)/shard_map/reduce_scatter | solution.py:46
  331.1 0.0 copy-done.1
  331.1 1.6 add_convert_fusion.1
  332.6 4.2 %all-to-all-start = ((bf16[8,16,512]{2,1,0:T(8,128)(2,1)}), bf16[8,16,512]{2,1,0:T(8,128)(2,1)S(1)}, u32[]{:S(2)}, u32[]{:S(2)}) async-start(bf16[8,16,512]{2,1,0:T(8,128)(2,1)} %bitcast), calls=%async_computation.2 | async-start | bytes 262144 | tf_op jit(solution)/shard_map/all_to_all | solution.py:60
  336.9 71.5 %reduce-scatter.11.cloned.1.call-done = bf16[128,512]{1,0:T(8,128)(2,1)} async-done(((bf16[2048,512]{1,0:T(8,128)(2,1)}), bf16[128,512]{1,0:T(8,128)(2,1)}) %reduce-scatter.11.cloned.1.call-update) | async-done | bytes 131088 | tf_op jit(solution)/shard_map/reduce_scatter | solution.py:46
  408.4 0.0 copy-done.2
  408.4 1.6 add_convert_fusion
  410.0 0.0 all-to-all-done
  410.0 0.7 copy.10
Async XLA Ops:
  7.2 50.8 %copy-start = (bf16[1024,512]{1,0:T(8,128)(2,1)S(1)}, bf16[1024,512]{1,0:T(8,128)(2,1)}, u32[]{:S(2)}) copy-start(bf16[1024,512]{1,0:T(8,128)(2,1)} %param.6) | copy-start | bytes 3145732
  7.2 50.8 %all-gather.9.cloned.1.call-start = ((), (), s32[]{:S(2)}) async-start(), calls=%async_computation.9 | async-start | bytes 2228224 | tf_op jit(solution)/shard_map/all_gather | solution.py:14
  7.9 96.7 %all-gather.5.cloned.1.call-start = ((), (), s32[]{:S(2)}) async-start(), calls=%async_computation.5 | async-start | bytes 2228224 | tf_op jit(solution)/shard_map/all_gather | solution.py:14
  8.7 135.6 %reduce-scatter.9.cloned.1.call-start = ((), (), s32[]{:S(2)}) async-start(), calls=%async_computation.10 | async-start | bytes 4718592 | tf_op jit(solution)/shard_map/reduce_scatter | solution.py:34
  63.9 40.8 %copy-start.3 = (bf16[512,1024]{1,0:T(8,128)(2,1)S(1)}, bf16[512,1024]{1,0:T(8,128)(2,1)}, u32[]{:S(2)}) copy-start(bf16[512,1024]{1,0:T(8,128)(2,1)} %param.5) | copy-start | bytes 3145732
  63.9 119.3 %reduce-scatter.5.cloned.1.call-start = ((), (), s32[]{:S(2)}) async-start(), calls=%async_computation.6 | async-start | bytes 4718592 | tf_op jit(solution)/shard_map/reduce_scatter | solution.py:34
  110.6 108.4 %all-gather.7.cloned.1.call-start = ((), (), s32[]{:S(2)}) async-start(), calls=%async_computation.7 | async-start | bytes 4718592 | tf_op jit(solution)/shard_map/all_gather | solution.py:18
  187.8 65.5 %all-gather.11.cloned.1.call-start = ((), (), s32[]{:S(2)}) async-start(), calls=%async_computation.11 | async-start | bytes 4718592 | tf_op jit(solution)/shard_map/all_gather | solution.py:18
  188.3 142.7 %reduce-scatter.7.cloned.1.call-start = ((), (), s32[]{:S(2)}) async-start(), calls=%async_computation.8 | async-start | bytes 2228224 | tf_op jit(solution)/shard_map/reduce_scatter | solution.py:46
  224.9 183.5 %reduce-scatter.11.cloned.1.call-start = ((), (), s32[]{:S(2)}) async-start(), calls=%async_computation.12 | async-start | bytes 2228224 | tf_op jit(solution)/shard_map/reduce_scatter | solution.py:46
  266.2 64.9 %copy-start.1 = (bf16[128,512]{1,0:T(8,128)(2,1)S(1)}, bf16[128,512]{1,0:T(8,128)(2,1)}, u32[]{:S(2)}) copy-start(bf16[128,512]{1,0:T(8,128)(2,1)} %param.4) | copy-start | bytes 393220
  266.2 142.2 %copy-start.2 = (bf16[128,512]{1,0:T(8,128)(2,1)S(1)}, bf16[128,512]{1,0:T(8,128)(2,1)}, u32[]{:S(2)}) copy-start(bf16[128,512]{1,0:T(8,128)(2,1)} %param.7) | copy-start | bytes 393220
  332.6 77.4 %all-to-all-start = ((bf16[8,16,512]{2,1,0:T(8,128)(2,1)}), bf16[8,16,512]{2,1,0:T(8,128)(2,1)S(1)}, u32[]{:S(2)}, u32[]{:S(2)}) async-start(bf16[8,16,512]{2,1,0:T(8,128)(2,1)} %bitcast), calls=%async_computation.2 | async-start | bytes 262144 | tf_op jit(solution)/shard_map/all_to_all | solution.py:60
Sparse Core Ops, SparseCore 0:
  10.2 47.7 all-gather.8
  60.1 44.5 all-gather.4
  107.1 37.1 reduce-scatter.8
  146.5 36.6 reduce-scatter.4
  187.9 31.0 all-gather.6
  221.2 32.0 all-gather.10
  256.5 74.5 reduce-scatter.6
  334.7 73.7 reduce-scatter.10
where the time goes:
time: 418 us
  waiting for transfers between devices  353 us (84%)
  matrix products  35.4 us (8%)
  between operations  14.2 us (3%)
  other arithmetic  7.74 us (2%)
  starting transfers between devices  4.75 us (1%)
    reduce_scatter x2, waiting for transfers between devices, unit_sum(): lax.psum_scatter(unit_term().astype(jnp.bfloat16), 'row', scatter_dimensi...  130 us
    all_gather x2, waiting for transfers between devices, token_panel(): return lax.all_gather(local_rows, 'row', axis=0, tiled=True)  89.9 us
    reduce_scatter x2, waiting for transfers between devices, width_split(): lax.psum_scatter(width_term().astype(jnp.bfloat16), 'col', scatter_dimens...  72.5 us
    all_gather x2, waiting for transfers between devices, hidden_panel(): return lax.all_gather(local_rows, 'col', axis=0, tiled=True)  58.7 us
    dot_general x2, matrix products, contract_last(): lax.dot_general(left, right, (((1,), (1,)), ((), ())), preferred_element_...  11.8 us
  transfers between devices with their start and end apart: 9, of which 8 were waited for; matrix products, arithmetic and copies ran while one was open for 10% of the time, Pallas kernels for 0%

commit v1 on v0

--- a/solution.py
+++ b/solution.py
@@ -11,7 +11,15 @@
 
 
 def token_panel(local_rows):
-    return lax.all_gather(local_rows, "row", axis=0, tiled=True)
+    return jnp.concatenate(
+        jax.lax.all_to_all(
+            jnp.stack([local_rows for _ in range(jax.lax.axis_size("row"))], 0),
+            concat_axis=0,
+            axis_name="row",
+            split_axis=0,
+        ),
+        0,
+    )
 
 
 def hidden_panel(local_rows):

time: 418 us -> 359 us (0.86)
  waiting for transfers between devices: 353 us -> 225 us
  blocking collectives: 0 us -> 67.2 us
  local copies, waits for them, and re-layouts: 2.5 us -> 7.09 us
    all_gather x2 -> x0, waiting for transfers between devices: 89.9 us -> none  [token_panel(): return lax.all_gather(local_rows, 'row', axis=0, tiled=True)]
    all_to_all x0 -> x2, blocking collectives: none -> 67.2 us  [token_panel(): jax.lax.all_to_all(jnp.stack([local_rows for _ in range(jax.lax.axis_size...]
    reduce_scatter x2, waiting for transfers between devices: 72.5 us -> 38 us  [width_split(): lax.psum_scatter(width_term().astype(jnp.bfloat16), 'col', scatter_dimens...]
  transfers between devices with their start and end apart: 9 -> 7, of which waited for: 8 -> 5; matrix products, arithmetic and copies ran while one was open for 10% -> 10% of each run, Pallas kernels for 0% -> 0%
where the time goes in v1:
time: 359 us
  waiting for transfers between devices  225 us (63%)
  blocking collectives  67.2 us (19%)
  matrix products  33.2 us (9%)
  between operations  14.2 us (4%)
  other arithmetic  7.74 us (2%)
  local copies, waits for them, and re-layouts  7.09 us (2%)
  starting transfers between devices  4.67 us (1%)
    reduce_scatter x2, waiting for transfers between devices, unit_sum(): lax.psum_scatter(unit_term().astype(jnp.bfloat16), 'row', scatter_dimensi...  128 us
    all_to_all x2, blocking collectives, token_panel(): jax.lax.all_to_all(jnp.stack([local_rows for _ in range(jax.lax.axis_size...  67.2 us
    all_gather x2, waiting for transfers between devices, hidden_panel(): return lax.all_gather(local_rows, 'col', axis=0, tiled=True)  58.6 us
    reduce_scatter x2, waiting for transfers between devices, width_split(): lax.psum_scatter(width_term().astype(jnp.bfloat16), 'col', scatter_dimens...  38 us
    dot_general x2, matrix products, contract_last(): lax.dot_general(left, right, (((1,), (1,)), ((), ())), preferred_element_...  10.5 us
  transfers between devices with their start and end apart: 7, of which 5 were waited for; matrix products, arithmetic and copies ran while one was open for 10% of the time, Pallas kernels for 0%

profile of v1, /device:TPU:0, one launch (start us, length us, event | category | flops | bytes accessed | tf_op | source)
XLA Modules:
  0.0 358.7 jit_solution(18397980137955862737)
XLA Ops:
  7.2 0.0 copy-start
  7.2 0.0 reduce-scatter.9.cloned.1.call-start
  7.2 1.2 stack.5
  8.4 36.2 %all_to_all.29 = bf16[16,128,512]{2,1,0:T(8,128)(2,1)S(1)} all-to-all(bf16[16,128,512]{2,1,0:T(8,128)(2,1)S(1)} %stack.5), channel_id=1, replica_groups=mesh['row'=16,'col'=8] {'row'}, dimensions={0} | all-to-all | bytes 4194304 | tf_op jit(solution)/shard_map/all_to_all | solution.py:15
  44.6 0.0 copy-done
  44.6 4.3 %convolution_convert_fusion = bf16[2048,1024]{1,0:T(8,128)(2,1)} fusion(bf16[2048,512]{1,0:T(8,128)(2,1)S(1)} %bitcast.20, bf16[1024,512]{1,0:T(8,128)(2,1)S(1)} %copy-done), kind=kOutput, calls=%fused_computation | convolution fusion | flops 2149580800 | bytes 7340032 | tf_op jit(solution)/shard_map/dot_general | solution.py:30
  48.9 0.0 copy-start.2
  48.9 0.0 reduce-scatter.9.cloned.1.call-update
  48.9 0.0 reduce-scatter.5.cloned.1.call-start
  49.0 0.8 copy-done.2
  49.8 0.2 stack.4
  50.0 0.0 copy-start.4
  50.0 31.0 %all_to_all.30 = bf16[16,128,512]{2,1,0:T(8,128)(2,1)S(1)} all-to-all(bf16[16,128,512]{2,1,0:T(8,128)(2,1)S(1)} %stack.4), channel_id=1, replica_groups=mesh['row'=16,'col'=8] {'row'}, dimensions={0} | all-to-all | bytes 4194304 | tf_op jit(solution)/shard_map/all_to_all | solution.py:15
  81.0 0.0 copy-start.1
  81.0 1.3 copy-done.1
  82.3 0.0 copy-done.4
  82.3 4.3 %convolution_convert_fusion.1 = bf16[2048,1024]{1,0:T(8,128)(2,1)} fusion(bf16[2048,512]{1,0:T(8,128)(2,1)S(1)} %bitcast.22, bf16[512,1024]{1,0:T(8,128)(2,1)S(1)} %copy-done.4), kind=kOutput, calls=%fused_computation.1 | convolution fusion | flops 2149580800 | bytes 7340032 | tf_op jit(solution)/shard_map/dot_general | solution.py:40
  86.7 0.0 reduce-scatter.5.cloned.1.call-update
  86.7 0.0 all-gather.3.cloned.1.call-start
  86.7 0.0 reduce-scatter.9.cloned.1.call-done
  86.8 38.0 %reduce-scatter.5.cloned.1.call-done = bf16[256,1024]{1,0:T(8,128)(2,1)} async-done(((bf16[2048,1024]{1,0:T(8,128)(2,1)}), bf16[256,1024]{1,0:T(8,128)(2,1)}) %reduce-scatter.5.cloned.1.call-update) | async-done | bytes 524304 | tf_op jit(solution)/shard_map/reduce_scatter | solution.py:42
  124.7 4.6 %fusion.38 = (bf16[256,1024]{1,0:T(8,128)(2,1)}, bf16[256,1024]{1,0:T(8,128)(2,1)}) fusion(bf16[256,1024]{1,0:T(8,128)(2,1)} %reduce-scatter.5.cloned.1.call-done, bf16[256,1024]{1,0:T(8,128)(2,1)} %reduce-scatter.9.cloned.1.call-done), kind=kLoop, calls=%fused_computation.50 | loop fusion | flops 20185088 | bytes 2097152 | tf_op jit(solution)/shard_map/convert_element_type | solution.py:65
  129.3 0.0 all-gather.3.cloned.1.call-update
  129.3 0.0 all-gather.5.cloned.1.call-start
  129.4 0.5 all-gather.5.cloned.1.call-update
  129.9 0.0 reduce-scatter.7.cloned.1.call-start
  129.9 30.5 %all-gather.3.cloned.1.call-done = bf16[2048,1024]{1,0:T(8,128)(2,1)} async-done(((bf16[256,1024]{1,0:T(8,128)(2,1)}), bf16[2048,1024]{1,0:T(8,128)(2,1)}) %all-gather.3.cloned.1.call-update) | async-done | bytes 4194320 | tf_op jit(solution)/shard_map/all_gather | solution.py:26
  160.4 5.9 %convolution_convert_fusion.3 = bf16[2048,512]{1,0:T(8,128)(2,1)} fusion(bf16[2048,1024]{1,0:T(8,128)(2,1)} %all-gather.3.cloned.1.call-done, bf16[1024,512]{1,0:T(8,128)(2,1)S(1)} %copy-done), kind=kOutput, calls=%fused_computation.3 | convolution fusion | flops 2148532224 | bytes 7340032 | tf_op jit(solution)/shard_map/dot_general | solution.py:52
  166.3 0.0 reduce-scatter.7.cloned.1.call-update
  166.4 0.2 reduce-scatter.11.cloned.1.call-start
  166.6 28.1 %all-gather.5.cloned.1.call-done = bf16[2048,1024]{1,0:T(8,128)(2,1)} async-done(((bf16[256,1024]{1,0:T(8,128)(2,1)}), bf16[2048,1024]{1,0:T(8,128)(2,1)}) %all-gather.5.cloned.1.call-update) | async-done | bytes 4194320 | tf_op jit(solution)/shard_map/all_gather | solution.py:26
  194.7 6.2 %convolution_convert_fusion.2 = bf16[2048,512]{1,0:T(8,128)(2,1)} fusion(bf16[2048,1024]{1,0:T(8,128)(2,1)} %all-gather.5.cloned.1.call-done, bf16[512,1024]{1,0:T(8,128)(2,1)} %param.5), kind=kOutput, calls=%fused_computation.2 | convolution fusion | flops 2148532224 | bytes 7340032 | tf_op jit(solution)/shard_map/dot_general | solution.py:30
  200.9 0.0 reduce-scatter.11.cloned.1.call-update
  200.9 6.6 %convolution_bitcast_fusion = f32[512,1024]{0,1:T(8,128)} fusion(bf16[2048,1024]{1,0:T(8,128)(2,1)} %all-gather.5.cloned.1.call-done, bf16[2048,512]{1,0:T(8,128)(2,1)} %bitcast.23), kind=kOutput, calls=%fused_computation.10 | convolution fusion | flops 2147483648 | bytes 8388608 | tf_op jit(solution)/shard_map/dot_general | solution.py:72
  207.4 2.9 copy.9
  210.3 0.0 copy-start.3
  210.3 5.9 %fusion.39 = f32[1024,512]{1,0:T(8,128)} fusion(bf16[2048,1024]{1,0:T(8,128)(2,1)} %all-gather.3.cloned.1.call-done, bf16[2048,512]{1,0:T(8,128)(2,1)S(1)} %bitcast.21), kind=kOutput, calls=%fused_computation.53 | convolution fusion | flops 2147483648 | bytes 8388608 | tf_op jit(solution)/shard_map/dot_general | solution.py:69
  216.2 56.1 %reduce-scatter.7.cloned.1.call-done = bf16[128,512]{1,0:T(8,128)(2,1)} async-done(((bf16[2048,512]{1,0:T(8,128)(2,1)}), bf16[128,512]{1,0:T(8,128)(2,1)}) %reduce-scatter.7.cloned.1.call-update) | async-done | bytes 131088 | tf_op jit(solution)/shard_map/reduce_scatter | solution.py:54
  272.4 1.6 add_convert_fusion.1
  274.0 4.2 %all-to-all-start.1 = ((bf16[8,16,512]{2,1,0:T(8,128)(2,1)}), bf16[8,16,512]{2,1,0:T(8,128)(2,1)S(1)}, u32[]{:S(2)}, u32[]{:S(2)}) async-start(bf16[8,16,512]{2,1,0:T(8,128)(2,1)} %bitcast.1), calls=%async_computation.3 | async-start | bytes 262144 | tf_op jit(solution)/shard_map/all_to_all | solution.py:68
  278.2 71.4 %reduce-scatter.11.cloned.1.call-done = bf16[128,512]{1,0:T(8,128)(2,1)} async-done(((bf16[2048,512]{1,0:T(8,128)(2,1)}), bf16[128,512]{1,0:T(8,128)(2,1)}) %reduce-scatter.11.cloned.1.call-update) | async-done | bytes 131088 | tf_op jit(solution)/shard_map/reduce_scatter | solution.py:54
  349.6 0.0 copy-done.3
  349.6 1.6 add_convert_fusion
  351.2 0.0 all-to-all-done.1
  351.2 0.7 copy.10
Async XLA Ops:
  7.2 37.4 %copy-start = (bf16[1024,512]{1,0:T(8,128)(2,1)S(1)}, bf16[1024,512]{1,0:T(8,128)(2,1)}, u32[]{:S(2)}) copy-start(bf16[1024,512]{1,0:T(8,128)(2,1)} %param.6) | copy-start | bytes 3145732
  7.2 79.6 %reduce-scatter.9.cloned.1.call-start = ((), (), s32[]{:S(2)}) async-start(), calls=%async_computation.10 | async-start | bytes 4718592 | tf_op jit(solution)/shard_map/reduce_scatter | solution.py:42
  48.9 0.9 copy-start.2
  48.9 75.8 %reduce-scatter.5.cloned.1.call-start = ((), (), s32[]{:S(2)}) async-start(), calls=%async_computation.7 | async-start | bytes 4718592 | tf_op jit(solution)/shard_map/reduce_scatter | solution.py:42
  50.0 32.3 %copy-start.4 = (bf16[512,1024]{1,0:T(8,128)(2,1)S(1)}, bf16[512,1024]{1,0:T(8,128)(2,1)}, u32[]{:S(2)}) copy-start(bf16[512,1024]{1,0:T(8,128)(2,1)} %param.5) | copy-start | bytes 3145732
  81.0 1.3 copy-start.1
  86.7 73.8 %all-gather.3.cloned.1.call-start = ((), (), s32[]{:S(2)}) async-start(), calls=%async_computation.8 | async-start | bytes 4718592 | tf_op jit(solution)/shard_map/all_gather | solution.py:26
  129.3 65.4 %all-gather.5.cloned.1.call-start = ((), (), s32[]{:S(2)}) async-start(), calls=%async_computation.11 | async-start | bytes 4718592 | tf_op jit(solution)/shard_map/all_gather | solution.py:26
  129.9 142.5 %reduce-scatter.7.cloned.1.call-start = ((), (), s32[]{:S(2)}) async-start(), calls=%async_computation.9 | async-start | bytes 2228224 | tf_op jit(solution)/shard_map/reduce_scatter | solution.py:54
  166.4 183.2 %reduce-scatter.11.cloned.1.call-start = ((), (), s32[]{:S(2)}) async-start(), calls=%async_computation.12 | async-start | bytes 2228224 | tf_op jit(solution)/shard_map/reduce_scatter | solution.py:54
  210.3 139.3 %copy-start.3 = (bf16[128,512]{1,0:T(8,128)(2,1)S(1)}, bf16[128,512]{1,0:T(8,128)(2,1)}, u32[]{:S(2)}) copy-start(bf16[128,512]{1,0:T(8,128)(2,1)} %param.7) | copy-start | bytes 393220
  274.0 77.2 %all-to-all-start.1 = ((bf16[8,16,512]{2,1,0:T(8,128)(2,1)}), bf16[8,16,512]{2,1,0:T(8,128)(2,1)S(1)}, u32[]{:S(2)}, u32[]{:S(2)}) async-start(bf16[8,16,512]{2,1,0:T(8,128)(2,1)} %bitcast.1), calls=%async_computation.3 | async-start | bytes 262144 | tf_op jit(solution)/shard_map/all_to_all | solution.py:68
Sparse Core Ops, SparseCore 0:
  49.1 36.7 reduce-scatter.8
  88.2 36.4 reduce-scatter.4
  129.4 30.9 all-gather.2
  162.6 32.0 all-gather.4
  197.8 74.5 reduce-scatter.6
  275.9 73.7 reduce-scatter.10
